TPU v7x, 32 devices: a whole 2x2x4 slice. The times are simulated.
32 devices in a mesh: expert: 8 (over z, y), tensor: 4 (over x, core).
Axes of the slice: x: 2, y: 2, z: 4, core: 2. Of those that a mesh axis runs over, the one named last changes fastest.
Arguments:
- inputs: bfloat16 [12608, 512], P('expert'), may hold values from -6 to 6
- gain_attend: float32 [512], replicated, may hold values from 0.25 to 1.75
- triple_weight: bfloat16 [512, 3, 512], P(None, None, 'tensor'), may hold values from -0.25 to 0.25
- project_weight: bfloat16 [512, 512], P('tensor'), may hold values from -1.5 to 1.5
- gain_mixture: float32 [512], replicated, may hold values from 0.25 to 1.75
- router_weight: bfloat16 [512, 16], replicated, may hold values from -0.125 to 0.125
- expert_first: bfloat16 [16, 512, 2048], P('expert', None, 'tensor'), may hold values from -0.25 to 0.25
- expert_second: bfloat16 [16, 2048, 512], P('expert', 'tensor'), may hold values from -0.1875 to 0.1875
- triple_down: bfloat16 [512, 128], replicated, may hold values from -0.25 to 0.25
- triple_up: bfloat16 [128, 3, 512], P(None, None, 'tensor'), may hold values from -1.5 to 1.5
- project_down: bfloat16 [512, 128], P('tensor'), may hold values from -1.5 to 1.5
- project_up: bfloat16 [128, 512], replicated, may hold values from -1.5 to 1.5
- router_down: bfloat16 [512, 128], replicated, may hold values from -0.25 to 0.25
- router_up: bfloat16 [128, 16], replicated, may hold values from -0.75 to 0.75
- first_down: bfloat16 [512, 128], replicated, may hold values from -0.25 to 0.25
- first_up: bfloat16 [128, 2048], P(None, 'tensor'), may hold values from -1.5 to 1.5
- second_down: bfloat16 [2048, 128], P('tensor'), may hold values from -0.1875 to 0.1875
- second_up: bfloat16 [128, 512], replicated, may hold values from -1.5 to 1.5
- adapter_index: int32 [64], P('expert'), may hold values from 0 to 7
- routes: int32 [12608, 2], P('expert'), may hold values from 0 to 15, all different within a row
- priority: int32 [8, 1576], P('expert'), may hold values from 0 to 1575, each once within a row
- cotangent: bfloat16 [12608, 512], P('expert'), may hold values from -6 to 6
Outputs:
- block_output: bfloat16 [12608, 512], P('expert')
- input_grad: bfloat16 [12608, 512], P('expert')
- triple_down_grad: float32 [512, 128], replicated
- triple_up_grad: float32 [128, 3, 512], P(None, None, 'tensor')
- project_down_grad: float32 [512, 128], P('tensor')
- project_up_grad: float32 [128, 512], replicated
- router_down_grad: float32 [512, 128], replicated
- router_up_grad: float32 [128, 16], replicated
- first_down_grad: float32 [512, 128], replicated
- first_up_grad: float32 [128, 2048], P(None, 'tensor')
- second_down_grad: float32 [2048, 128], P('tensor')
- second_up_grad: float32 [128, 512], replicated
Inputs may be any that keep to these rules, and one draw needn't show every extreme that they name: `routes`: each row names 2 different experts. `priority`: each row holds every token index of its group once.
All inputs are finite; a program needn't handle non-finite values.
Results may differ from a plain program's by a relative error of at most 0.028.
Values may be sent and summed in bfloat16 or wider, within the bound.
A program may use at most 192 MiB of HBM per device.

v0:
```python
import jax
import jax.numpy as jnp
from jax import lax
from jax.sharding import PartitionSpec as P

HEAD_DIM = 64
TOP = 2
ADAPTERS = 8
RANK = 16
highest = lax.Precision.HIGHEST
norm_eps = 1e-06


def norm_rows(values, gain):
    centre = jnp.mean(values, axis=-1, keepdims=True)
    shifted = values - centre
    spread = jnp.mean(shifted * shifted, axis=-1, keepdims=True)
    return shifted * lax.rsqrt(spread + norm_eps) * gain


def pick_columns(token_ids):
    column = jnp.arange(ADAPTERS * RANK, dtype=jnp.int32) // RANK
    return (token_ids[:, None] == column[None, :]).astype(jnp.float32)


def place_pairs(route_rows, ranking, capacity, experts):
    count = ranking.shape[0]
    ranked = route_rows[ranking]
    pair_expert = jnp.concatenate([ranked[:, 0], ranked[:, 1]])
    pair_token = jnp.concatenate([ranking, ranking])
    onehot = (pair_expert[:, None] == jnp.arange(experts, dtype=jnp.int32)[None, :]).astype(
        jnp.int32
    )
    position = jnp.sum(jnp.cumsum(onehot, axis=0) * onehot, axis=1) - 1
    kept_pair = position < capacity
    pair_slot = pair_expert * capacity + jnp.minimum(position, capacity - 1)
    target = jnp.where(kept_pair, pair_slot, experts * capacity)
    slot_token = (
        jnp.full((experts * capacity,), count, jnp.int32).at[target].set(pair_token, mode="drop")
    )
    slot_first = jnp.zeros((count,), jnp.int32).at[ranking].set(pair_slot[:count])
    slot_second = jnp.zeros((count,), jnp.int32).at[ranking].set(pair_slot[count:])
    keep_first = jnp.zeros((count,), jnp.int32).at[ranking].set(kept_pair[:count].astype(jnp.int32))
    keep_second = (
        jnp.zeros((count,), jnp.int32).at[ranking].set(kept_pair[count:].astype(jnp.int32))
    )
    return (
        slot_token,
        jnp.stack([slot_first, slot_second], axis=1),
        jnp.stack([keep_first, keep_second], axis=1),
    )


def to_experts(row_block, slot_ids):
    row_block, slot_ids = (
        lax.all_to_all(row_block, "expert", split_axis=0, concat_axis=0, tiled=True),
        lax.all_to_all(slot_ids, "expert", split_axis=0, concat_axis=0, tiled=True),
    )
    return (row_block, slot_ids)


def from_experts(partial_value):
    summed = lax.psum(partial_value.astype(jnp.bfloat16), "tensor")
    row_block = lax.all_to_all(summed, "expert", split_axis=0, concat_axis=0, tiled=True)
    return row_block


def body(
    inputs,
    gain_attend,
    triple_weight,
    project_weight,
    gain_mixture,
    router_weight,
    expert_first,
    expert_second,
    triple_down,
    triple_up,
    project_down,
    project_up,
    router_down,
    router_up,
    first_down,
    first_up,
    second_down,
    second_up,
    adapter_index,
    routes,
    priority,
    cotangent,
):
    f32 = jnp.float32
    bf16 = jnp.bfloat16
    tok_count, model_width = inputs.shape
    images = adapter_index.shape[0]
    seq_len = tok_count // images
    local_heads = triple_weight.shape[2] // HEAD_DIM
    local_width = triple_weight.shape[2]
    tensor_count = lax.axis_size("tensor")
    local_experts = expert_first.shape[0]
    experts = router_weight.shape[1]
    capacity = tensor_count * (
        (5 * tok_count * TOP + 4 * tensor_count * experts - 1) // (4 * tensor_count * experts)
    )
    score_scale = HEAD_DIM ** (-0.5)
    adapt_width = ADAPTERS * RANK
    token_ids = jnp.repeat(adapter_index, seq_len, total_repeat_length=tok_count)
    pick_cols = pick_columns(token_ids)
    source = inputs.astype(f32)
    normed1, norm1_back = jax.vjp(lambda values: norm_rows(values, gain_attend), source)
    attn_in = normed1.astype(bf16)
    triple_flat = triple_weight.reshape(model_width, 3 * local_width)
    triple_high = triple_up.reshape(adapt_width, 3 * local_width)
    triple_low = (jnp.dot(attn_in, triple_down, preferred_element_type=f32) * pick_cols).astype(
        bf16
    )
    triple = jnp.dot(attn_in, triple_flat, preferred_element_type=f32) + jnp.dot(
        triple_low, triple_high, preferred_element_type=f32
    )
    triple = triple.astype(bf16).reshape(images, seq_len, 3, local_heads, HEAD_DIM)
    queries = triple[:, :, 0]
    key_rows = triple[:, :, 1]
    value_rows = triple[:, :, 2]
    scores = (
        jnp.einsum("bqhd,bkhd->bhqk", queries, key_rows, preferred_element_type=f32) * score_scale
    )
    row_max = jnp.max(scores, axis=-1, keepdims=True)
    shifted = jnp.exp(scores - row_max)
    row_total = jnp.sum(shifted, axis=-1, keepdims=True)
    log_total = row_max + jnp.log(row_total)
    probs = (shifted / row_total).astype(bf16)
    attended = (
        jnp.einsum("bhqk,bkhd->bqhd", probs, value_rows, preferred_element_type=f32)
        .reshape(tok_count, local_width)
        .astype(bf16)
    )
    branch_part = jnp.dot(attended, project_weight, preferred_element_type=f32)
    project_part = jnp.dot(attended, project_down, preferred_element_type=f32)
    branch_sum, project_sum = (
        lax.psum(branch_part.astype(jnp.bfloat16), "tensor").astype(jnp.float32),
        lax.psum(project_part.astype(jnp.bfloat16), "tensor").astype(jnp.float32),
    )
    project_low = (project_sum * pick_cols).astype(bf16)
    middle = source + branch_sum + jnp.dot(project_low, project_up, preferred_element_type=f32)
    normed2, norm2_back = jax.vjp(lambda values: norm_rows(values, gain_mixture), middle)
    mixed_in = normed2.astype(bf16)
    router_low = jnp.dot(mixed_in, router_down, preferred_element_type=f32) * pick_cols
    logits = jnp.dot(mixed_in, router_weight, preferred_element_type=f32) + jnp.dot(
        router_low, router_up.astype(f32), precision=highest
    )
    chosen = (routes[:, :, None] == jnp.arange(experts, dtype=jnp.int32)[None, None, :]).astype(f32)
    picked = jnp.sum(chosen * logits[:, None, :], axis=-1)
    gate_prob = jax.nn.softmax(picked, axis=-1)
    slot_token, slot_pairs, keep_pairs = place_pairs(routes, priority[0], capacity, experts)
    keep_float = keep_pairs.astype(f32)
    gate_wts = gate_prob * keep_float
    padded = jnp.concatenate([mixed_in, jnp.zeros((1, model_width), bf16)], axis=0)
    send_rows = padded[slot_token].reshape(experts, capacity, model_width)
    id_pad = jnp.concatenate([token_ids, jnp.zeros((1,), jnp.int32)])
    send_ids = id_pad[slot_token].reshape(experts, capacity)
    got_rows, got_ids = to_experts(send_rows, send_ids)
    sources = got_rows.shape[0] // local_experts
    got = got_rows.reshape(sources, local_experts, capacity, model_width)
    got_cols = pick_columns(got_ids.reshape(-1)).reshape(
        sources, local_experts, capacity, adapt_width
    )
    first_low = (
        jnp.einsum("necd,dr->necr", got, first_down, preferred_element_type=f32) * got_cols
    ).astype(bf16)
    pre = jnp.einsum("necd,edf->necf", got, expert_first, preferred_element_type=f32) + jnp.einsum(
        "necr,rf->necf", first_low, first_up, preferred_element_type=f32
    )
    hidden_val, gelu_back = jax.vjp(lambda values: jax.nn.gelu(values, approximate=False), pre)
    hidden = hidden_val.astype(bf16)
    second_low = (
        jnp.einsum("necf,fr->necr", hidden, second_down, preferred_element_type=f32) * got_cols
    ).astype(bf16)
    part_out = jnp.einsum(
        "necf,efd->necd", hidden, expert_second, preferred_element_type=f32
    ) + jnp.einsum("necr,rd->necd", second_low, second_up, preferred_element_type=f32)
    back_rows = from_experts(part_out.reshape(sources * local_experts, capacity, model_width))
    flat_rows = back_rows.reshape(experts * capacity, model_width)
    fetched = flat_rows[slot_pairs].astype(f32)
    block_output = (middle + jnp.sum(gate_wts[:, :, None] * fetched, axis=1)).astype(bf16)
    grad_out = cotangent.astype(f32)
    grad_gate = jnp.sum(fetched * grad_out[:, None, :], axis=-1) * keep_float
    pair_target = jnp.where(keep_pairs > 0, slot_pairs, experts * capacity)
    slot_gate = jnp.zeros((experts * capacity,), f32).at[pair_target].set(gate_wts, mode="drop")
    grad_pad = jnp.concatenate([cotangent, jnp.zeros((1, model_width), bf16)], axis=0)
    slot_grad = (
        (grad_pad[slot_token].astype(f32) * slot_gate[:, None])
        .astype(bf16)
        .reshape(experts, capacity, model_width)
    )
    got_grad, grad_ids = to_experts(slot_grad, send_ids)
    grad_res = got_grad.reshape(sources, local_experts, capacity, model_width)
    grad_cols = pick_columns(grad_ids.reshape(-1)).reshape(
        sources, local_experts, capacity, adapt_width
    )
    res_low = (
        jnp.einsum("necd,rd->necr", grad_res, second_up, preferred_element_type=f32) * grad_cols
    ).astype(bf16)
    grad_hidden = jnp.einsum(
        "necd,efd->necf", grad_res, expert_second, preferred_element_type=f32
    ) + jnp.einsum("necr,fr->necf", res_low, second_down, preferred_element_type=f32)
    grad_pre = gelu_back(grad_hidden)[0].astype(bf16)
    second_up_part = jnp.einsum("necr,necd->rd", second_low, grad_res, preferred_element_type=f32)
    second_down_part = jnp.einsum("necf,necr->fr", hidden, res_low, preferred_element_type=f32)
    first_up_part = jnp.einsum("necr,necf->rf", first_low, grad_pre, preferred_element_type=f32)
    pre_low = (
        jnp.einsum("necf,rf->necr", grad_pre, first_up, preferred_element_type=f32) * grad_cols
    ).astype(bf16)
    first_down_part = jnp.einsum("necd,necr->dr", got, pre_low, preferred_element_type=f32)
    grad_got = jnp.einsum(
        "necf,edf->necd", grad_pre, expert_first, preferred_element_type=f32
    ) + jnp.einsum("necr,dr->necd", pre_low, first_down, preferred_element_type=f32)
    back_grad = from_experts(grad_got.reshape(sources * local_experts, capacity, model_width))
    back_flat = back_grad.reshape(experts * capacity, model_width)
    grad_mixed = jnp.sum(back_flat[slot_pairs].astype(f32) * keep_float[:, :, None], axis=1)
    grad_picked = gate_prob * (grad_gate - jnp.sum(gate_prob * grad_gate, axis=-1, keepdims=True))
    grad_logits = jnp.sum(chosen * grad_picked[:, :, None], axis=1)
    logit_low = jnp.dot(grad_logits, router_up.astype(f32).T, precision=highest) * pick_cols
    grad_mixed = (
        grad_mixed
        + jnp.dot(grad_logits, router_weight.astype(f32).T, precision=highest)
        + jnp.dot(logit_low, router_down.astype(f32).T, precision=highest)
    )
    router_up_part = jnp.dot(router_low.T, grad_logits, precision=highest)
    router_down_part = jnp.dot(mixed_in.astype(f32).T, logit_low, precision=highest)
    grad_middle = grad_out + norm2_back(grad_mixed)[0]
    grad_branch = grad_middle.astype(bf16)
    project_up_part = jnp.dot(project_low.T, grad_branch, preferred_element_type=f32)
    branch_low = (
        jnp.dot(grad_branch, project_up.T, preferred_element_type=f32) * pick_cols
    ).astype(bf16)
    project_down_part = jnp.dot(attended.T, branch_low, preferred_element_type=f32)
    grad_attended = (
        jnp.dot(grad_branch, project_weight.T, preferred_element_type=f32)
        + jnp.dot(branch_low, project_down.T, preferred_element_type=f32)
    ).astype(bf16)
    grad_heads = grad_attended.reshape(images, seq_len, local_heads, HEAD_DIM)
    again = (
        jnp.einsum("bqhd,bkhd->bhqk", queries, key_rows, preferred_element_type=f32) * score_scale
    )
    probs_again = jnp.exp(again - log_total)
    grad_probs = jnp.einsum("bqhd,bkhd->bhqk", grad_heads, value_rows, preferred_element_type=f32)
    grad_values = jnp.einsum(
        "bhqk,bqhd->bkhd", probs_again.astype(bf16), grad_heads, preferred_element_type=f32
    )
    inner = jnp.sum(probs_again * grad_probs, axis=-1, keepdims=True)
    grad_scores = (probs_again * (grad_probs - inner)).astype(bf16)
    grad_queries = (
        jnp.einsum("bhqk,bkhd->bqhd", grad_scores, key_rows, preferred_element_type=f32)
        * score_scale
    )
    grad_keys = (
        jnp.einsum("bhqk,bqhd->bkhd", grad_scores, queries, preferred_element_type=f32)
        * score_scale
    )
    grad_triple = (
        jnp.stack([grad_queries, grad_keys, grad_values], axis=2)
        .reshape(tok_count, 3 * local_width)
        .astype(bf16)
    )
    triple_up_part = jnp.dot(triple_low.T, grad_triple, preferred_element_type=f32).reshape(
        adapt_width, 3, local_width
    )
    triple_grad_low = jnp.dot(grad_triple, triple_high.T, preferred_element_type=f32) * pick_cols
    triple_down_part = jnp.dot(attn_in.T, triple_grad_low.astype(bf16), preferred_element_type=f32)
    grad_in_part = jnp.dot(grad_triple, triple_flat.T, preferred_element_type=f32) + jnp.dot(
        triple_grad_low.astype(bf16), triple_down.T, preferred_element_type=f32
    )
    grad_attn_in = lax.psum(grad_in_part.astype(jnp.bfloat16), "tensor").astype(jnp.float32)
    input_grad = (grad_middle + norm1_back(grad_attn_in)[0]).astype(bf16)
    (
        triple_up_grad,
        project_down_grad,
        project_up_grad,
        router_down_grad,
        router_up_grad,
        first_up_grad,
        second_down_grad,
    ) = lax.psum(
        (
            triple_up_part,
            project_down_part,
            project_up_part,
            router_down_part,
            router_up_part,
            first_up_part,
            second_down_part,
        ),
        "expert",
    )
    triple_down_grad, first_down_grad, second_up_grad = lax.psum(
        (triple_down_part, first_down_part, second_up_part), ("expert", "tensor")
    )
    return (
        block_output,
        input_grad,
        triple_down_grad,
        triple_up_grad,
        project_down_grad,
        project_up_grad,
        router_down_grad,
        router_up_grad,
        first_down_grad,
        first_up_grad,
        second_down_grad,
        second_up_grad,
    )


def solution(mesh):
    return jax.shard_map(
        body,
        mesh=mesh,
        in_specs=(
            P("expert", None),
            P(),
            P(None, None, "tensor"),
            P("tensor", None),
            P(),
            P(),
            P("expert", None, "tensor"),
            P("expert", "tensor", None),
            P(),
            P(None, None, "tensor"),
            P("tensor", None),
            P(),
            P(),
            P(),
            P(),
            P(None, "tensor"),
            P("tensor", None),
            P(),
            P("expert"),
            P("expert", None),
            P("expert", None),
            P("expert", None),
        ),
        out_specs=(
            P("expert", None),
            P("expert", None),
            P(),
            P(None, None, "tensor"),
            P("tensor", None),
            P(),
            P(),
            P(),
            P(),
            P(None, "tensor"),
            P("tensor", None),
            P(),
        ),
        check_vma=False,
    )
```

profile of v0, /device:TPU:0, one launch (start us, length us, event | category | flops | bytes accessed | tf_op | source)
XLA Modules:
  0.0 1132.3 jit_solution(9242527268222042039)
XLA Ops:
  16.5 5.2 select_select_fusion
  57.8 8.8 scatter_custom_fusion.3
  66.6 8.8 scatter_custom_fusion.4
  75.4 9.0 scatter_custom_fusion
  84.5 8.8 scatter_custom_fusion.1
  99.0 15.8 %scatter_custom_fusion.2 = s32[3968]{0:T(1024)S(1)} fusion(s32[3152]{0:T(1024)S(1)} %fusion.105, s32[3152]{0:T(1024)S(1)} %pad_add_fusion.1, s32[]{:T(128)} %constant.191.clone.1), kind=kCustom, calls=%fused_computation.210 | custom fusion | bytes 15876 | tf_op jit(solution)/shard_map/scatter | solution.py:39
  114.9 12.4 %gather_fusion.4 = bf16[3968,512]{1,0:T(8,128)(2,1)} fusion(bf16[1577,512]{1,0:T(8,128)(2,1)S(1)} %concatenate.76, s32[4096]{0:T(1024)S(1)} %pad_clamp_fusion.1), kind=kCustom, calls=%fused_computation.4 | custom fusion | bytes 8142336 | tf_op jit(solution)/shard_map/gather | solution.py:191
  136.4 16.0 %scatter_custom_fusion.5 = f32[3968]{0:T(1024)S(1)} fusion(s32[3152]{0:T(1024)} %reshape.722, f32[3152]{0:T(1024)S(1)} %reshape.724, f32[]{:T(128)} %constant.180.clone.1), kind=kCustom, calls=%fused_computation.208 | custom fusion | bytes 16384 | tf_op jit(solution)/shard_map/scatter | solution.py:188
  156.5 7.7 all-to-all-start.3
  165.8 12.4 %gather_fusion.1 = bf16[3968,512]{1,0:T(8,128)(2,1)} fusion(bf16[1577,512]{1,0:T(8,128)(2,1)S(1)} %concatenate.72, s32[4096]{0:T(1024)S(1)} %pad_clamp_fusion.1), kind=kCustom, calls=%fused_computation.1 | custom fusion | bytes 8142336 | tf_op jit(solution)/shard_map/gather | solution.py:158
  178.2 76.5 %all-to-all-done.3 = bf16[16,248,512]{2,1,0:T(8,128)(2,1)} async-done(((bf16[16,248,512]{2,1,0:T(8,128)(2,1)}), bf16[16,248,512]{2,1,0:T(8,128)(2,1)}, u32[]{:S(2)}, u32[]{:S(2)}) %all-to-all-start.3) | async-done | bytes 4063264 | tf_op jit(solution)/shard_map/all_to_all | solution.py:56
  259.3 20.9 %gather_fusion.2 = s32[3968]{0:T(1024)S(1)} fusion(s32[1577]{0:T(1024)S(1)} %pad_add_fusion.2, s32[4096]{0:T(1024)S(1)} %pad_clamp_fusion.1), kind=kCustom, calls=%fused_computation.2 | custom fusion | bytes 47616 | tf_op jit(solution)/shard_map/gather | solution.py:160
  280.9 7.6 fusion.19
  288.5 60.5 %all-to-all-done = bf16[16,248,512]{2,1,0:T(8,128)(2,1)} async-done(((bf16[16,248,512]{2,1,0:T(8,128)(2,1)}), bf16[16,248,512]{2,1,0:T(8,128)(2,1)}, u32[]{:S(2)}, u32[]{:S(2)}) %all-to-all-start) | async-done | bytes 4063264 | tf_op jit(solution)/shard_map/all_to_all | solution.py:56
  352.7 7.6 fusion.23
  363.8 6.7 fusion.44
  370.5 19.2 %multiply_convert_fusion = (bf16[8,2,248,512]{3,2,0,1:T(8,128)(2,1)S(1)}, f32[8,2,248,512]{3,2,0,1:T(8,128)}) fusion(f32[8,2,248,512]{3,2,0,1:T(8,128)S(1)} %get-tuple-element.75, u8[2,248,512]{2,1,0:T(8,128)(4,1)S(1)} %get-tuple-element.25, u8[2,248,512]{2,1,0:T(8,128)(4,1)S(1)} %get-tuple-element.24), kind=kLoop, calls=%fused_computation.28 | loop fusion | flops 142213120 | bytes 20824064 | tf_op jit(solution)/shard_map/convert_element_type | solution.py:174
  389.8 4.9 fusion.41
  394.7 8.2 add_convert_fusion
  418.1 150.5 %all-reduce.19.cloned.1.call-done = (bf16[16,248,512]{2,1,0:T(8,128)(2,1)}, bf16[16,248,512]{2,1,0:T(8,128)(2,1)}) async-done(((bf16[16,248,512]{2,1,0:T(8,128)(2,1)}, bf16[16,248,512]{2,1,0:T(8,128)(2,1)}), (bf16[16,248,512]{2,1,0:T(8,128)(2,1)}, bf16[16,248,512]{2,1,0:T(8,128)(2,1)})) %all-reduce.19.cloned.1.call-update) | async-done | bytes 8126480 | tf_op jit(solution)/shard_map/psum | solution.py:63
  568.7 96.2 %all_to_all.30 = bf16[16,248,512]{2,1,0:T(8,128)(2,1)} all-to-all(bf16[16,248,512]{2,1,0:T(8,128)(2,1)} %get-tuple-element.39), channel_id=1, replica_groups=mesh['expert'=8,'tensor'=4] {'expert'}, dimensions={0} | all-to-all | bytes 8126464 | tf_op jit(solution)/shard_map/all_to_all | solution.py:64
  686.8 13.5 %gather_fusion.3 = bf16[3152,512]{1,0:T(8,128)(2,1)} fusion(bf16[3968,512]{1,0:T(8,128)(2,1)} %bitcast.214, s32[4096]{0:T(1024)S(1)} %pad_clamp_fusion), kind=kCustom, calls=%fused_computation.3 | custom fusion | bytes 6467904 | tf_op jit(solution)/shard_map/gather | solution.py:183
  700.3 7.9 reshape.734
  708.2 21.8 %multiply_reduce_fusion = (f32[1576,2]{1,0:T(8,128)}, f32[1576,512]{1,0:T(8,128)}) fusion(f32[1576,2,512]{2,1,0:T(2,128)} %reshape.734, f32[1576,512]{1,0:T(8,128)} %convert_element_type.195, f32[1576,2]{1,0:T(8,128)S(1)} %copy.191), kind=kLoop, calls=%fused_computation.41 | loop fusion | flops 5645232 | bytes 12935808 | tf_op jit(solution)/shard_map/reduce_sum | solution.py:186
  731.5 27.1 %all-to-all-done.4 = bf16[16,248,512]{2,1,0:T(8,128)(2,1)} async-done(((bf16[16,248,512]{2,1,0:T(8,128)(2,1)}), bf16[16,248,512]{2,1,0:T(8,128)(2,1)}, u32[]{:S(2)}, u32[]{:S(2)}) %all-to-all-start.4) | async-done | bytes 4063264 | tf_op jit(solution)/shard_map/all_to_all | solution.py:64
  758.7 13.1 %gather_fusion.5 = bf16[3152,512]{1,0:T(8,128)(2,1)} fusion(bf16[3968,512]{1,0:T(8,128)(2,1)} %bitcast.41, s32[4096]{0:T(1024)S(1)} %pad_clamp_fusion), kind=kCustom, calls=%fused_computation.5 | custom fusion | bytes 6467904 | tf_op jit(solution)/shard_map/gather | solution.py:219
  771.8 7.9 reshape.735
  780.6 35.1 %multiply_reduce_fusion.1 = f32[1576,512]{1,0:T(8,128)S(1)} fusion(f32[1576,2,512]{2,1,0:T(2,128)} %reshape.735, f32[1576,2]{1,0:T(8,128)S(1)} %copy.207), kind=kLoop, calls=%fused_computation.42 | loop fusion | flops 2420736 | bytes 9695552 | tf_op jit(solution)/shard_map/reduce_sum | solution.py:219
  850.9 20.3 %psum.115 = f32[128,16]{0,1:T(8,128)} all-reduce(f32[128,16]{0,1:T(8,128)S(1)} %fusion.144), channel_id=1, replica_groups=mesh['expert'=8,'tensor'=4] {'expert'}, use_global_device_ids=true, to_apply=%region_38.39 | all-reduce | flops 2048 | bytes 16384 | tf_op jit(solution)/shard_map/psum | solution.py:283
  875.6 10.3 all-reduce.13.cloned.1.call-done
  894.2 127.9 %all-reduce.15.cloned.1.call-done = (f32[512,128]{1,0:T(8,128)}, f32[512,128]{1,0:T(8,128)}, f32[128,512]{1,0:T(8,128)}) async-done(((f32[512,128]{1,0:T(8,128)}, f32[512,128]{1,0:T(8,128)}, f32[128,512]{1,0:T(8,128)}), (f32[512,128]{1,0:T(8,128)}, f32[512,128]{1,0:T(8,128)}, f32[128,512]{1,0:T(8,128)})) %all-reduce.15.cloned.1.call-update) | async-done | bytes 786448 | tf_op jit(solution)/shard_map/psum | solution.py:295
  1022.1 90.5 %all-reduce.17.cloned.1.call-done = (f32[128,3,128]{2,0,1:T(8,128)}, f32[128,128]{1,0:T(8,128)}, f32[128,512]{1,0:T(8,128)}, f32[512,128]{1,0:T(8,128)}, f32[128,512]{1,0:T(8,128)}, /*index=5*/f32[512,128]{1,0:T(8,128)}) async-done(((f32[128,3,128]{2,0,1:T(8,128)}, f32[128,128]{1,0:T(8,128)}, f32[128,512]{1,0:T(8,128)}, f32[512,128]{1,0:T(8,128)}, f32[128,512]{1,0:T(8,128)}, ...) | async-done | bytes 1310736 | tf_op jit(solution)/shard_map/psum | solution.py:283
  (374 shorter events, 177.3 us)
Async XLA Ops:
  7.2 345.5 %copy-start = (bf16[2,512,512]{2,1,0:T(8,128)(2,1)S(1)}, bf16[2,512,512]{2,1,0:T(8,128)(2,1)}, u32[]{:S(2)}) copy-start(bf16[2,512,512]{2,1,0:T(8,128)(2,1)} %param.30) | copy-start | bytes 3145732
  7.2 120.1 %all-reduce.21.cloned.1.call-start = ((), (), s32[]{:S(2)}) async-start(), calls=%async_computation.9 | async-start | bytes 4034560 | tf_op jit(solution)/shard_map/psum | solution.py:140
  7.3 14.4 %copy-start.89 = (s32[128]{0:T(128)}, s32[128]{0:T(128)S(1)}, u32[]{:S(2)}) copy-start(s32[128]{0:T(128)S(1)} %and_select_fusion) | copy-start | bytes 1540
  114.9 12.4 %copy-start.67 = (bf16[128,512]{1,0:T(8,128)(2,1)S(1)}, bf16[128,512]{1,0:T(8,128)(2,1)}, u32[]{:S(2)}) copy-start(bf16[128,512]{1,0:T(8,128)(2,1)} %param.35) | copy-start | bytes 393220
  114.9 12.4 %copy-start.90 = (s32[128]{0:T(128)S(1)}, s32[128]{0:T(128)}, u32[]{:S(2)}) copy-start(s32[128]{0:T(128)} %copy-done.89) | copy-start | bytes 1540
  156.5 98.1 %all-to-all-start.3 = ((bf16[16,248,512]{2,1,0:T(8,128)(2,1)}), bf16[16,248,512]{2,1,0:T(8,128)(2,1)}, u32[]{:S(2)}, u32[]{:S(2)}) async-start(bf16[16,248,512]{2,1,0:T(8,128)(2,1)} %fusion.1), calls=%async_computation.3 | async-start | bytes 8126464 | tf_op jit(solution)/shard_map/all_to_all | solution.py:56
  254.7 94.3 %all-to-all-start = ((bf16[16,248,512]{2,1,0:T(8,128)(2,1)}), bf16[16,248,512]{2,1,0:T(8,128)(2,1)}, u32[]{:S(2)}, u32[]{:S(2)}) async-start(bf16[16,248,512]{2,1,0:T(8,128)(2,1)} %bitcast.219), calls=%async_computation | async-start | bytes 8126464 | tf_op jit(solution)/shard_map/all_to_all | solution.py:56
  259.3 21.6 %copy-start.30 = (bf16[2,512,512]{2,1,0:T(8,128)(2,1)S(1)}, bf16[2,512,512]{2,1,0:T(8,128)(2,1)}, u32[]{:S(2)}) copy-start(bf16[2,512,512]{2,1,0:T(8,128)(2,1)} %param.31) | copy-start | bytes 3145732
  349.0 11.3 all-to-all-start.1
  352.6 216.0 %all-reduce.19.cloned.1.call-start = ((), (), s32[]{:S(2)}) async-start(), calls=%async_computation.8 | async-start | bytes 16252928 | tf_op jit(solution)/shard_map/psum | solution.py:63
  363.8 30.9 %slice-start = ((s8[8126464]{0:T(1024)(128)(4,1)}), s8[4194304]{0:T(1024)(128)(4,1)S(1)}, s32[]{:S(2)}) async-start(s8[8126464]{0:T(1024)(128)(4,1)} %bitcast.220), calls=%async_computation.10 | async-start | bytes 8388608
  370.5 19.2 %copy-start.21 = (f32[8,2,248,512]{3,2,0,1:T(8,128)}, f32[8,2,248,512]{3,2,0,1:T(8,128)S(1)}, u32[]{:S(2)}) copy-start(f32[8,2,248,512]{3,2,0,1:T(8,128)S(1)} %get-tuple-element.75) | copy-start | bytes 24379396
  370.5 19.2 %copy-start.60 = (bf16[128,512]{1,0:T(8,128)(2,1)S(1)}, bf16[128,512]{1,0:T(8,128)(2,1)}, u32[]{:S(2)}) copy-start(bf16[128,512]{1,0:T(8,128)(2,1)} %param.41) | copy-start | bytes 393220
  370.5 24.1 %slice-start.1 = ((s8[8126464]{0:T(1024)(128)(4,1)}), s8[3932160]{0:T(1024)(128)(4,1)S(1)}, s32[]{:S(2)}) async-start(s8[8126464]{0:T(1024)(128)(4,1)} %bitcast.220), calls=%async_computation.11 | async-start | bytes 7864320
  389.8 23.2 %copy-start.15 = (bf16[8,2,248,512]{3,2,0,1:T(8,128)(2,1)}, bf16[8,2,248,512]{3,2,0,1:T(8,128)(2,1)S(1)}, u32[]{:S(2)}) copy-start(bf16[8,2,248,512]{3,2,0,1:T(8,128)(2,1)S(1)} %get-tuple-element.47) | copy-start | bytes 12189700
  394.6 8.2 copy-start.102
  664.9 93.8 %all-to-all-start.4 = ((bf16[16,248,512]{2,1,0:T(8,128)(2,1)}), bf16[16,248,512]{2,1,0:T(8,128)(2,1)}, u32[]{:S(2)}, u32[]{:S(2)}) async-start(bf16[16,248,512]{2,1,0:T(8,128)(2,1)} %get-tuple-element.40), calls=%async_computation.4 | async-start | bytes 8126464 | tf_op jit(solution)/shard_map/all_to_all | solution.py:64
  669.6 216.3 %all-reduce.13.cloned.1.call-start = ((), (), s32[]{:S(2)}) async-start(), calls=%async_computation.5 | async-start | bytes 3227648 | tf_op jit(solution)/shard_map/psum | solution.py:273
  708.2 23.2 %copy-start.72 = (f32[1576,2]{0,1:T(2,128)S(1)}, f32[1576,2]{0,1:T(2,128)}, u32[]{:S(2)}) copy-start(f32[1576,2]{0,1:T(2,128)} %get-tuple-element.46) | copy-start | bytes 37828
  708.2 23.3 %copy-start.71 = (s32[1576,2]{0,1:T(2,128)S(1)}, s32[1576,2]{0,1:T(2,128)}, u32[]{:S(2)}) copy-start(s32[1576,2]{0,1:T(2,128)} %param.43) | copy-start | bytes 37828
  731.5 84.2 %copy-start.35 = (f32[1576,16]{0,1:T(8,128)}, f32[1576,16]{0,1:T(8,128)S(1)}, u32[]{:S(2)}) copy-start(f32[1576,16]{0,1:T(8,128)S(1)} %select_reduce_fusion) | copy-start | bytes 302596
  780.6 35.1 %copy-start.78 = (bf16[512,16]{0,1:T(8,128)(2,1)S(1)}, bf16[512,16]{0,1:T(8,128)(2,1)}, u32[]{:S(2)}) copy-start(bf16[512,16]{0,1:T(8,128)(2,1)} %param.29) | copy-start | bytes 49156
  843.6 178.5 %all-reduce.15.cloned.1.call-start = ((), (), s32[]{:S(2)}) async-start(), calls=%async_computation.6 | async-start | bytes 1572864 | tf_op jit(solution)/shard_map/psum | solution.py:295
  850.0 36.0 %copy-start.7 = (bf16[1576,512]{1,0:T(8,128)(2,1)S(1)}, bf16[1576,512]{1,0:T(8,128)(2,1)}, u32[]{:S(2)}) copy-start(bf16[1576,512]{1,0:T(8,128)(2,1)} %param.24) | copy-start | bytes 4841476
  850.0 36.0 %copy-start.55 = (f32[1576]{0:T(1024)S(1)}, f32[1576]{0:T(1024)}, u32[]{:S(2)}) copy-start(f32[1576]{0:T(1024)} %copy-done.54) | copy-start | bytes 18916
  850.0 36.0 %copy-start.84 = (f32[512]{0:T(512)S(1)}, f32[512]{0:T(512)}, u32[]{:S(2)}) copy-start(f32[512]{0:T(512)} %param.25) | copy-start | bytes 6148
  850.0 262.7 %all-reduce.17.cloned.1.call-start = ((), (), s32[]{:S(2)}) async-start(), calls=%async_computation.7 | async-start | bytes 2621440 | tf_op jit(solution)/shard_map/psum | solution.py:283
  871.2 17.2 %copy-start.74 = (f32[1576]{0:T(1024)S(1)}, f32[1576]{0:T(1024)}, u32[]{:S(2)}) copy-start(f32[1576]{0:T(1024)} %copy-done.73) | copy-start | bytes 18916
  871.2 17.2 %copy-start.62 = (f32[1576]{0:T(1024)S(1)}, f32[1576]{0:T(1024)}, u32[]{:S(2)}) copy-start(f32[1576]{0:T(1024)} %copy-done.61) | copy-start | bytes 18916
  891.4 234.2 %copy-start.1 = (bf16[2,512,512]{2,1,0:T(8,128)(2,1)S(1)}, bf16[2,512,512]{2,1,0:T(8,128)(2,1)}, u32[]{:S(2)}) copy-start(bf16[2,512,512]{2,1,0:T(8,128)(2,1)} %param.30) | copy-start | bytes 3145732
  1022.1 102.7 %copy-start.56 = (f32[128,512]{1,0:T(8,128)S(1)}, f32[128,512]{1,0:T(8,128)}, u32[]{:S(2)}) copy-start(f32[128,512]{1,0:T(8,128)} %get-tuple-element.91) | copy-start | bytes 786436
  1112.6 11.5 %copy-start.57 = (f32[512,128]{1,0:T(8,128)S(1)}, f32[512,128]{1,0:T(8,128)}, u32[]{:S(2)}) copy-start(f32[512,128]{1,0:T(8,128)} %get-tuple-element.90) | copy-start | bytes 786436
  (83 other events, 261.7 us)
Sparse Core Ops, SparseCore 0:
  47.1 53.1 all-reduce.20
  418.3 150.3 all-reduce.18
  843.7 42.1 all-reduce.12
  891.9 130.2 all-reduce.14
  1028.0 84.5 all-reduce.16
where the time goes:
time: 1140 us; the launch traced here: 1130 us
  waiting for transfers between devices  543 us (48%)
  local copies, waits for them, and re-layouts  219 us (19%)
  blocking collectives  117 us (10%)
  other arithmetic  114 us (10%)
  matrix products  102 us (9%)
  starting transfers between devices  20.8 us (2%)
  between operations  15.9 us (1%)
    psum x1, waiting for transfers between devices, from_experts(): summed = lax.psum(partial_value.astype(jnp.bfloat16), 'tensor')  151 us
    all_to_all x2, waiting for transfers between devices, to_experts(): lax.all_to_all(row_block, 'expert', split_axis=0, concat_axis=0, tiled=True)  137 us
    psum x1, waiting for transfers between devices, body(): lax.psum((triple_down_part, first_down_part, second_up_part), ('expert',...  128 us
    all_to_all x1, blocking collectives, from_experts(): lax.all_to_all(summed, 'expert', split_axis=0, concat_axis=0, tiled=True)  96.2 us
    psum x1, waiting for transfers between devices, body(): lax.psum((triple_up_part, project_down_part, project_up_part, router_down...  90.5 us
    reduce_sum x1, other arithmetic, body(): jnp.sum(back_flat[slot_pairs].astype(f32) * keep_float[:, :, None], axis=1)  35.1 us
    unnamed x229, local copies, waits for them, and re-layouts  28.4 us
    all_to_all x1, waiting for transfers between devices, from_experts(): lax.all_to_all(summed, 'expert', split_axis=0, concat_axis=0, tiled=True)  27.1 us
  transfers between devices with their start and end apart: 9, of which 7 were waited for; matrix products, arithmetic and copies ran while one was open for 19% of the time, Pallas kernels for 0%

commit v1 on v0

--- a/solution.py
+++ b/solution.py
@@ -60,7 +60,7 @@
 
 
 def from_experts(partial_value):
-    summed = lax.psum(partial_value.astype(jnp.bfloat16), "tensor")
+    summed = jnp.sum(lax.all_gather(partial_value.astype(jnp.bfloat16), "tensor"), axis=0)
     row_block = lax.all_to_all(summed, "expert", split_axis=0, concat_axis=0, tiled=True)
     return row_block
 

time: 1140 us -> 1100 us (0.965)
  blocking collectives: 117 us -> 20.5 us
  other arithmetic: 114 us -> 149 us
  local copies, waits for them, and re-layouts: 219 us -> 232 us
    all_gather x0 -> x2, waiting for transfers between devices: none -> 181 us  [from_experts(): lax.all_gather(partial_value.astype(jnp.bfloat16), 'tensor')]
    psum x1 -> x0, waiting for transfers between devices: 151 us -> none  [from_experts(): summed = lax.psum(partial_value.astype(jnp.bfloat16), 'tensor')]
    all_to_all x1 -> x0, blocking collectives: 96.2 us -> none  [from_experts(): lax.all_to_all(summed, 'expert', split_axis=0, concat_axis=0, tiled=True)]
    all_to_all x2, waiting for transfers between devices: 137 us -> 72.5 us  [to_experts(): lax.all_to_all(row_block, 'expert', split_axis=0, concat_axis=0, tiled=True)]
    all_to_all x1 -> x2, waiting for transfers between devices: 27.1 us -> 52.4 us  [from_experts(): lax.all_to_all(summed, 'expert', split_axis=0, concat_axis=0, tiled=True)]
    reduce_sum x0 -> x2, other arithmetic: none -> 23.7 us  [from_experts(): jnp.sum(lax.all_gather(partial_value.astype(jnp.bfloat16), 'tensor'), axi...]
    unnamed x229 -> x221, local copies, waits for them, and re-layouts: 28.4 us -> 28.9 us
  transfers between devices with their start and end apart: 9 -> 11, of which waited for: 7 -> 9; matrix products, arithmetic and copies ran while one was open for 19% -> 23% of each run, Pallas kernels for 0% -> 0%
where the time goes in v1:
time: 1100 us; the launch traced here: 1090 us
  waiting for transfers between devices  537 us (49%)
  local copies, waits for them, and re-layouts  232 us (21%)
  other arithmetic  149 us (14%)
  matrix products  109 us (10%)
  starting transfers between devices  25 us (2%)
  blocking collectives  20.5 us (2%)
  between operations  16 us (1%)
    all_gather x2, waiting for transfers between devices, from_experts(): lax.all_gather(partial_value.astype(jnp.bfloat16), 'tensor')  181 us
    psum x1, waiting for transfers between devices, body(): lax.psum((triple_down_part, first_down_part, second_up_part), ('expert',...  128 us
    psum x1, waiting for transfers between devices, body(): lax.psum((triple_up_part, project_down_part, project_up_part, router_down...  90.5 us
    all_to_all x2, waiting for transfers between devices, to_experts(): lax.all_to_all(row_block, 'expert', split_axis=0, concat_axis=0, tiled=True)  72.5 us
    all_to_all x2, waiting for transfers between devices, from_experts(): lax.all_to_all(summed, 'expert', split_axis=0, concat_axis=0, tiled=True)  52.4 us
    reduce_sum x1, other arithmetic, body(): jnp.sum(back_flat[slot_pairs].astype(f32) * keep_float[:, :, None], axis=1)  35.1 us
    unnamed x221, local copies, waits for them, and re-layouts  28.9 us
    reduce_sum x2, other arithmetic, from_experts(): jnp.sum(lax.all_gather(partial_value.astype(jnp.bfloat16), 'tensor'), axi...  23.7 us
  transfers between devices with their start and end apart: 11, of which 9 were waited for; matrix products, arithmetic and copies ran while one was open for 23% of the time, Pallas kernels for 0%

profile of v1, /device:TPU:0, one launch (start us, length us, event | category | flops | bytes accessed | tf_op | source)
XLA Modules:
  0.0 1088.4 jit_solution(14208265031094504052)
XLA Ops:
  61.4 9.6 reduce-window.14
  82.2 16.1 %scatter_custom_fusion.2 = s32[3968]{0:T(1024)S(1)} fusion(s32[3152]{0:T(1024)S(1)} %fusion.105, s32[3152]{0:T(1024)S(1)} %pad_add_fusion.1, s32[]{:T(128)} %constant.193.clone.1), kind=kCustom, calls=%fused_computation.210 | custom fusion | bytes 15876 | tf_op jit(solution)/shard_map/scatter | solution.py:39
  98.3 6.1 all-reduce.17.cloned.1.call-done
  110.9 12.4 %gather_fusion.1 = bf16[3968,512]{1,0:T(8,128)(2,1)} fusion(bf16[1577,512]{1,0:T(8,128)(2,1)S(1)} %concatenate.72, s32[4096]{0:T(1024)S(1)} %pad_clamp_fusion.1), kind=kCustom, calls=%fused_computation.1 | custom fusion | bytes 8142336 | tf_op jit(solution)/shard_map/gather | solution.py:158
  128.8 8.9 scatter_custom_fusion.1
  137.8 8.9 scatter_custom_fusion
  148.3 12.4 %gather_fusion.4 = bf16[3968,512]{1,0:T(8,128)(2,1)} fusion(bf16[1577,512]{1,0:T(8,128)(2,1)S(1)} %concatenate.76, s32[4096]{0:T(1024)S(1)} %pad_clamp_fusion.1), kind=kCustom, calls=%fused_computation.4 | custom fusion | bytes 8142336 | tf_op jit(solution)/shard_map/gather | solution.py:191
  160.8 8.9 scatter_custom_fusion.3
  169.7 9.3 scatter_custom_fusion.4
  187.2 15.8 %scatter_custom_fusion.5 = f32[3968]{0:T(1024)S(1)} fusion(s32[3152]{0:T(1024)S(1)} %reshape.742, f32[3152]{0:T(1024)S(1)} %reshape.744, f32[]{:T(128)} %constant.182.clone.1), kind=kCustom, calls=%fused_computation.208 | custom fusion | bytes 15876 | tf_op jit(solution)/shard_map/scatter | solution.py:188
  207.2 12.0 %all-to-all-done = bf16[16,248,512]{2,1,0:T(8,128)(2,1)} async-done(((bf16[16,248,512]{2,1,0:T(8,128)(2,1)}), bf16[16,248,512]{2,1,0:T(8,128)(2,1)}, u32[]{:S(2)}, u32[]{:S(2)}) %all-to-all-start) | async-done | bytes 4063264 | tf_op jit(solution)/shard_map/all_to_all | solution.py:56
  223.8 20.9 %gather_fusion.2 = s32[3968]{0:T(1024)S(1)} fusion(s32[1577]{0:T(1024)S(1)} %pad_add_fusion.2, s32[4096]{0:T(1024)S(1)} %pad_clamp_fusion.1), kind=kCustom, calls=%fused_computation.2 | custom fusion | bytes 47616 | tf_op jit(solution)/shard_map/gather | solution.py:160
  245.4 7.6 fusion.23
  253.1 60.4 %all-to-all-done.3 = bf16[16,248,512]{2,1,0:T(8,128)(2,1)} async-done(((bf16[16,248,512]{2,1,0:T(8,128)(2,1)}), bf16[16,248,512]{2,1,0:T(8,128)(2,1)}, u32[]{:S(2)}, u32[]{:S(2)}) %all-to-all-start.3) | async-done | bytes 4063264 | tf_op jit(solution)/shard_map/all_to_all | solution.py:56
  317.2 7.7 fusion.19
  328.3 6.7 fusion.44
  335.1 19.4 %multiply_convert_fusion = (bf16[8,2,248,512]{3,2,0,1:T(8,128)(2,1)}, f32[8,2,248,512]{3,2,0,1:T(8,128)}) fusion(f32[8,2,248,512]{3,2,0,1:T(8,128)S(1)} %get-tuple-element.73, u8[2,248,512]{2,1,0:T(8,128)(4,1)S(1)} %get-tuple-element.25, u8[2,248,512]{2,1,0:T(8,128)(4,1)S(1)} %get-tuple-element.24), kind=kLoop, calls=%fused_computation.28 | loop fusion | flops 142213120 | bytes 20824064 | tf_op jit(solution)/shard_map/convert_element_type | solution.py:174
  358.0 8.2 add_convert_fusion
  383.2 94.1 %all-gather.5.cloned.1.call-done = bf16[4,16,248,512]{3,2,1,0:T(8,128)(2,1)} async-done(((bf16[1,16,248,512]{3,2,1,0:T(8,128)(2,1)}), bf16[4,16,248,512]{3,2,1,0:T(8,128)(2,1)}) %all-gather.5.cloned.1.call-update) | async-done | bytes 16252944 | tf_op jit(solution)/shard_map/all_gather | solution.py:63
  477.3 12.2 %reduce_sum.212 = bf16[16,248,512]{2,1,0:T(8,128)(2,1)} reduce(bf16[4,16,248,512]{3,2,1,0:T(8,128)(2,1)} %all-gather.5.cloned.1.call-done, bf16[]{:T(256)} %constant.196.clone.1), dimensions={0}, to_apply=%region_22.23 | reduce | flops 6094848 | bytes 20316162 | tf_op jit(solution)/shard_map/reduce_sum | solution.py:63
  494.9 87.0 %all-gather.3.cloned.1.call-done = bf16[4,16,248,512]{3,2,1,0:T(8,128)(2,1)} async-done(((bf16[1,16,248,512]{3,2,1,0:T(8,128)(2,1)}), bf16[4,16,248,512]{3,2,1,0:T(8,128)(2,1)}) %all-gather.3.cloned.1.call-update) | async-done | bytes 16252944 | tf_op jit(solution)/shard_map/all_gather | solution.py:63
  581.9 11.5 %reduce_sum.210 = bf16[16,248,512]{2,1,0:T(8,128)(2,1)} reduce(bf16[4,16,248,512]{3,2,1,0:T(8,128)(2,1)} %all-gather.3.cloned.1.call-done, bf16[]{:T(256)} %constant.196.clone.1), dimensions={0}, to_apply=%region_17.18 | reduce | flops 6094848 | bytes 20316162 | tf_op jit(solution)/shard_map/reduce_sum | solution.py:63
  616.2 13.5 %gather_fusion.5 = bf16[3152,512]{1,0:T(8,128)(2,1)} fusion(bf16[3968,512]{1,0:T(8,128)(2,1)} %bitcast.41, s32[4096]{0:T(1024)S(1)} %pad_clamp_fusion), kind=kCustom, calls=%fused_computation.5 | custom fusion | bytes 6467904 | tf_op jit(solution)/shard_map/gather | solution.py:219
  629.7 7.9 reshape.755
  637.6 52.4 %all-to-all-done.2 = bf16[16,248,512]{2,1,0:T(8,128)(2,1)} async-done(((bf16[16,248,512]{2,1,0:T(8,128)(2,1)}), bf16[16,248,512]{2,1,0:T(8,128)(2,1)}, u32[]{:S(2)}, u32[]{:S(2)}) %all-to-all-start.2) | async-done | bytes 4063264 | tf_op jit(solution)/shard_map/all_to_all | solution.py:64
  690.0 13.1 %gather_fusion.3 = bf16[3152,512]{1,0:T(8,128)(2,1)} fusion(bf16[3968,512]{1,0:T(8,128)(2,1)} %bitcast.31, s32[4096]{0:T(1024)S(1)} %pad_clamp_fusion), kind=kCustom, calls=%fused_computation.3 | custom fusion | bytes 6467904 | tf_op jit(solution)/shard_map/gather | solution.py:183
  703.1 7.9 reshape.754
  711.0 21.8 %multiply_reduce_fusion = (f32[1576,2]{1,0:T(8,128)}, f32[1576,512]{1,0:T(8,128)}) fusion(f32[1576,2,512]{2,1,0:T(2,128)} %reshape.754, f32[1576,512]{1,0:T(8,128)} %convert_element_type.213, f32[1576,2]{1,0:T(8,128)S(1)} %copy.191), kind=kLoop, calls=%fused_computation.41 | loop fusion | flops 5645232 | bytes 12935808 | tf_op jit(solution)/shard_map/reduce_sum | solution.py:186
  735.4 35.1 %multiply_reduce_fusion.1 = f32[1576,512]{1,0:T(8,128)S(1)} fusion(f32[1576,2,512]{2,1,0:T(2,128)} %reshape.755, f32[1576,2]{1,0:T(8,128)S(1)} %copy.207), kind=kLoop, calls=%fused_computation.42 | loop fusion | flops 2420736 | bytes 9695552 | tf_op jit(solution)/shard_map/reduce_sum | solution.py:219
  811.0 20.5 %psum.99 = f32[128,16]{0,1:T(8,128)} all-reduce(f32[128,16]{0,1:T(8,128)S(1)} %fusion.144), channel_id=1, replica_groups=mesh['expert'=8,'tensor'=4] {'expert'}, use_global_device_ids=true, to_apply=%region_38.39 | all-reduce | flops 2048 | bytes 16384 | tf_op jit(solution)/shard_map/psum | solution.py:283
  849.9 127.9 %all-reduce.13.cloned.1.call-done = (f32[512,128]{1,0:T(8,128)}, f32[512,128]{1,0:T(8,128)}, f32[128,512]{1,0:T(8,128)}) async-done(((f32[512,128]{1,0:T(8,128)}, f32[512,128]{1,0:T(8,128)}, f32[128,512]{1,0:T(8,128)}), (f32[512,128]{1,0:T(8,128)}, f32[512,128]{1,0:T(8,128)}, f32[128,512]{1,0:T(8,128)})) %all-reduce.13.cloned.1.call-update) | async-done | bytes 786448 | tf_op jit(solution)/shard_map/psum | solution.py:295
  977.9 90.5 %all-reduce.15.cloned.1.call-done = (f32[128,3,128]{2,0,1:T(8,128)}, f32[128,128]{1,0:T(8,128)}, f32[128,512]{1,0:T(8,128)}, f32[512,128]{1,0:T(8,128)}, f32[128,512]{1,0:T(8,128)}, /*index=5*/f32[512,128]{1,0:T(8,128)}) async-done(((f32[128,3,128]{2,0,1:T(8,128)}, f32[128,128]{1,0:T(8,128)}, f32[128,512]{1,0:T(8,128)}, f32[512,128]{1,0:T(8,128)}, f32[128,512]{1,0:T(8,128)}, ...) | async-done | bytes 1310736 | tf_op jit(solution)/shard_map/psum | solution.py:283
  (372 shorter events, 225.4 us)
Async XLA Ops:
  7.2 238.3 %copy-start = (bf16[2,512,512]{2,1,0:T(8,128)(2,1)S(1)}, bf16[2,512,512]{2,1,0:T(8,128)(2,1)}, u32[]{:S(2)}) copy-start(bf16[2,512,512]{2,1,0:T(8,128)(2,1)} %param.30) | copy-start | bytes 3145732
  7.2 97.2 %all-reduce.17.cloned.1.call-start = ((), (), s32[]{:S(2)}) async-start(), calls=%async_computation.10 | async-start | bytes 4034560 | tf_op jit(solution)/shard_map/psum | solution.py:140
  58.3 20.5 %copy-start.75 = (s32[1576]{0:T(1024)}, s32[1576]{0:T(1024)S(1)}, u32[]{:S(2)}) copy-start(s32[1576]{0:T(1024)S(1)} %get-tuple-element.29) | copy-start | bytes 18916
  123.2 96.0 %all-to-all-start = ((bf16[16,248,512]{2,1,0:T(8,128)(2,1)}), bf16[16,248,512]{2,1,0:T(8,128)(2,1)}, u32[]{:S(2)}, u32[]{:S(2)}) async-start(bf16[16,248,512]{2,1,0:T(8,128)(2,1)} %bitcast.217), calls=%async_computation | async-start | bytes 8126464 | tf_op jit(solution)/shard_map/all_to_all | solution.py:56
  148.3 32.1 %copy-start.76 = (bf16[512,16]{0,1:T(8,128)(2,1)S(1)}, bf16[512,16]{0,1:T(8,128)(2,1)}, u32[]{:S(2)}) copy-start(bf16[512,16]{0,1:T(8,128)(2,1)} %param.29) | copy-start | bytes 49156
  160.7 21.7 %copy-start.43 = (bf16[512,128]{1,0:T(8,128)(2,1)S(1)}, bf16[512,128]{1,0:T(8,128)(2,1)}, u32[]{:S(2)}) copy-start(bf16[512,128]{1,0:T(8,128)(2,1)} %param.36) | copy-start | bytes 393220
  160.7 24.6 %copy-start.86 = (bf16[128,16]{0,1:T(8,128)(2,1)S(1)}, bf16[128,16]{0,1:T(8,128)(2,1)}, u32[]{:S(2)}) copy-start(bf16[128,16]{0,1:T(8,128)(2,1)} %param.37) | copy-start | bytes 12292
  219.2 94.3 %all-to-all-start.3 = ((bf16[16,248,512]{2,1,0:T(8,128)(2,1)}), bf16[16,248,512]{2,1,0:T(8,128)(2,1)}, u32[]{:S(2)}, u32[]{:S(2)}) async-start(bf16[16,248,512]{2,1,0:T(8,128)(2,1)} %fusion.1), calls=%async_computation.3 | async-start | bytes 8126464 | tf_op jit(solution)/shard_map/all_to_all | solution.py:56
  245.4 71.8 %copy-start.30 = (bf16[2,512,512]{2,1,0:T(8,128)(2,1)S(1)}, bf16[2,512,512]{2,1,0:T(8,128)(2,1)}, u32[]{:S(2)}) copy-start(bf16[2,512,512]{2,1,0:T(8,128)(2,1)} %param.31) | copy-start | bytes 3145732
  313.5 11.4 %all-to-all-start.1 = ((s32[8,2,248]{2,1,0:T(2,128)}), s32[8,2,248]{2,1,0:T(2,128)S(1)}, u32[]{:S(2)}, u32[]{:S(2)}) async-start(s32[8,2,248]{2,1,0:T(2,128)} %all_to_all.20), calls=%async_computation.1 | async-start | bytes 32768 | tf_op jit(solution)/shard_map/all_to_all | solution.py:57
  317.2 160.2 %all-gather.5.cloned.1.call-start = ((), (), s32[]{:S(2)}) async-start(), calls=%async_computation.6 | async-start | bytes 20316160 | tf_op jit(solution)/shard_map/all_gather | solution.py:63
  328.3 29.6 %slice-start = ((s8[8126464]{0:T(1024)(128)(4,1)}), s8[4194304]{0:T(1024)(128)(4,1)S(1)}, s32[]{:S(2)}) async-start(s8[8126464]{0:T(1024)(128)(4,1)} %bitcast.219), calls=%async_computation.11 | async-start | bytes 8388608
  335.1 19.4 %copy-start.21 = (f32[8,2,248,512]{3,2,0,1:T(8,128)}, f32[8,2,248,512]{3,2,0,1:T(8,128)S(1)}, u32[]{:S(2)}) copy-start(f32[8,2,248,512]{3,2,0,1:T(8,128)S(1)} %get-tuple-element.73) | copy-start | bytes 24379396
  335.1 19.4 %copy-start.58 = (bf16[128,512]{1,0:T(8,128)(2,1)S(1)}, bf16[128,512]{1,0:T(8,128)(2,1)}, u32[]{:S(2)}) copy-start(bf16[128,512]{1,0:T(8,128)(2,1)} %param.41) | copy-start | bytes 393220
  335.1 22.8 %slice-start.1 = ((s8[8126464]{0:T(1024)(128)(4,1)}), s8[3932160]{0:T(1024)(128)(4,1)S(1)}, s32[]{:S(2)}) async-start(s8[8126464]{0:T(1024)(128)(4,1)} %bitcast.219), calls=%async_computation.12 | async-start | bytes 7864320
  373.7 208.2 %all-gather.3.cloned.1.call-start = ((), (), s32[]{:S(2)}) async-start(), calls=%async_computation.5 | async-start | bytes 20316160 | tf_op jit(solution)/shard_map/all_gather | solution.py:63
  489.5 103.9 %all-to-all-start.4 = ((bf16[16,248,512]{2,1,0:T(8,128)(2,1)}), bf16[16,248,512]{2,1,0:T(8,128)(2,1)}, u32[]{:S(2)}, u32[]{:S(2)}) async-start(bf16[16,248,512]{2,1,0:T(8,128)(2,1)} %reduce_sum.212), calls=%async_computation.4 | async-start | bytes 8126464 | tf_op jit(solution)/shard_map/all_to_all | solution.py:64
  593.4 96.5 %all-to-all-start.2 = ((bf16[16,248,512]{2,1,0:T(8,128)(2,1)}), bf16[16,248,512]{2,1,0:T(8,128)(2,1)}, u32[]{:S(2)}, u32[]{:S(2)}) async-start(bf16[16,248,512]{2,1,0:T(8,128)(2,1)} %reduce_sum.210), calls=%async_computation.2 | async-start | bytes 8126464 | tf_op jit(solution)/shard_map/all_to_all | solution.py:64
  599.1 242.6 %all-reduce.11.cloned.1.call-start = ((), (), s32[]{:S(2)}) async-start(), calls=%async_computation.7 | async-start | bytes 3227648 | tf_op jit(solution)/shard_map/psum | solution.py:273
  711.0 23.3 %copy-start.68 = (f32[1576,2]{0,1:T(2,128)S(1)}, f32[1576,2]{0,1:T(2,128)}, u32[]{:S(2)}) copy-start(f32[1576,2]{0,1:T(2,128)} %get-tuple-element.44) | copy-start | bytes 37828
  735.3 36.7 %copy-start.23 = (f32[1576,128]{1,0:T(8,128)}, f32[1576,128]{1,0:T(8,128)S(1)}, u32[]{:S(2)}) copy-start(f32[1576,128]{1,0:T(8,128)S(1)} %convolution_select_fusion) | copy-start | bytes 2420740
  735.3 35.1 %copy-start.77 = (bf16[512,16]{0,1:T(8,128)(2,1)S(1)}, bf16[512,16]{0,1:T(8,128)(2,1)}, u32[]{:S(2)}) copy-start(bf16[512,16]{0,1:T(8,128)(2,1)} %param.29) | copy-start | bytes 49156
  799.6 178.3 %all-reduce.13.cloned.1.call-start = ((), (), s32[]{:S(2)}) async-start(), calls=%async_computation.8 | async-start | bytes 1572864 | tf_op jit(solution)/shard_map/psum | solution.py:295
  806.2 25.3 %copy-start.24 = (f32[1576,128]{1,0:T(8,128)S(1)}, f32[1576,128]{1,0:T(8,128)}, u32[]{:S(2)}) copy-start(f32[1576,128]{1,0:T(8,128)} %copy-done.23) | copy-start | bytes 2420740
  808.8 32.9 %copy-start.7 = (bf16[1576,512]{1,0:T(8,128)(2,1)S(1)}, bf16[1576,512]{1,0:T(8,128)(2,1)}, u32[]{:S(2)}) copy-start(bf16[1576,512]{1,0:T(8,128)(2,1)} %param.24) | copy-start | bytes 4841476
  808.8 32.9 %copy-start.51 = (f32[1576]{0:T(1024)S(1)}, f32[1576]{0:T(1024)}, u32[]{:S(2)}) copy-start(f32[1576]{0:T(1024)} %copy-done.50) | copy-start | bytes 18916
  808.8 32.9 %copy-start.84 = (f32[512]{0:T(512)S(1)}, f32[512]{0:T(512)}, u32[]{:S(2)}) copy-start(f32[512]{0:T(512)} %param.25) | copy-start | bytes 6148
  808.8 259.6 %all-reduce.15.cloned.1.call-start = ((), (), s32[]{:S(2)}) async-start(), calls=%async_computation.9 | async-start | bytes 2621440 | tf_op jit(solution)/shard_map/psum | solution.py:283
  831.5 12.7 %copy-start.72 = (f32[1576]{0:T(1024)S(1)}, f32[1576]{0:T(1024)}, u32[]{:S(2)}) copy-start(f32[1576]{0:T(1024)} %copy-done.71) | copy-start | bytes 18916
  831.5 12.8 %copy-start.61 = (f32[1576]{0:T(1024)S(1)}, f32[1576]{0:T(1024)}, u32[]{:S(2)}) copy-start(f32[1576]{0:T(1024)} %copy-done.60) | copy-start | bytes 18916
  847.1 234.1 %copy-start.1 = (bf16[2,512,512]{2,1,0:T(8,128)(2,1)S(1)}, bf16[2,512,512]{2,1,0:T(8,128)(2,1)}, u32[]{:S(2)}) copy-start(bf16[2,512,512]{2,1,0:T(8,128)(2,1)} %param.30) | copy-start | bytes 3145732
  977.9 102.7 %copy-start.52 = (f32[128,512]{1,0:T(8,128)S(1)}, f32[128,512]{1,0:T(8,128)}, u32[]{:S(2)}) copy-start(f32[128,512]{1,0:T(8,128)} %get-tuple-element.89) | copy-start | bytes 786436
  (81 other events, 266.4 us)
Sparse Core Ops, SparseCore 0:
  51.2 53.1 all-reduce.16
  373.8 103.4 all-gather.4
  478.9 102.9 all-gather.2
  799.7 41.8 all-reduce.10
  847.6 130.2 all-reduce.12
  983.8 84.5 all-reduce.14
